TPU v7x, 32 devices: a whole 2x2x4 slice. The times are simulated.
32 devices in a mesh: groups: 2 (over y), blk: 4 (over x, core), ulysses: 4 (over z).
Axes of the slice: x: 2, y: 2, z: 4, core: 2. Of those that a mesh axis runs over, the one named last changes fastest.
Arguments:
- query_proj: bfloat16 [1024, 1024], P(('groups', 'blk', 'ulysses')), parts along dimension 0, may hold values from -200 to 200
- key_proj: bfloat16 [1024, 1024], P(('groups', 'blk', 'ulysses')), parts along dimension 0, may hold values from -200 to 200
- value_proj: bfloat16 [1024, 1024], P(('groups', 'blk', 'ulysses')), parts along dimension 0, may hold values from -6 to 6
- query_gain: float32 [1024], replicated, may hold values from 1.2 to 2.4
- key_gain: float32 [1024], replicated, may hold values from 1.2 to 2.4
- control: bfloat16 [1024, 384], P(('groups', 'blk', 'ulysses')), parts along dimension 0, may hold values from -6 to 6
- hint_weight: bfloat16 [384, 1024], replicated, may hold values from -0.3125 to 0.3125
- hint_gain: float32 [8, 1024], replicated, may hold values from 0.3 to 3
- owner_map: int32 [32, 4], P(('groups', 'blk', 'ulysses')), parts along dimension 0, may hold values from 0 to 3, each once within a row
- layer_index: int32 [32], P(('groups', 'blk', 'ulysses')), parts along dimension 0, may hold values from 0 to 7
Outputs:
- block_out: bfloat16 [1024, 1024], P(('groups', 'blk', 'ulysses')), parts along dimension 0
There are 2 independent parts, one for each index of `groups`. A program takes and returns all parts, laid end to end along the dimension named above; an argument that names none is the same for every part. Nothing has to cross between parts.
Inputs may be any that keep to these rules, and one draw needn't show every extreme that they name: `owner_map`: each row is a permutation of 0 to 3.
All inputs are finite; a program needn't handle non-finite values.
Results may differ from a plain program's by a relative error of at most 0.008.
Values may be sent and summed in bfloat16 or wider, within the bound.
A program may use at most 64 MiB of HBM per device.

v0:
```python
import jax
import jax.numpy as jnp
from jax import lax
from jax.sharding import PartitionSpec as P

HEAD_DIM = 128


def normalize_rows(rows, gain):
    values = rows.astype(jnp.float32)
    scale = lax.rsqrt(jnp.mean(values * values, axis=-1, keepdims=True) + 1e-06)
    return (values * scale * gain).astype(jnp.bfloat16)


def block_size(count):
    block = min(count, 1024)
    while count % block:
        block = block - 1
    return block


def make_fold(queries):
    rows = queries.shape[0]
    heads = queries.shape[1] // HEAD_DIM
    shaped = queries.reshape(rows, heads, HEAD_DIM)
    factor = HEAD_DIM ** (-0.5)

    def update(state, pair):
        peak, totals, accum = state
        key_block, value_block = pair
        scores = (
            jnp.einsum("qhd,khd->hqk", shaped, key_block, preferred_element_type=jnp.float32)
            * factor
        )
        new_peak = jnp.maximum(peak, jnp.max(scores, axis=-1))
        correction = jnp.exp(peak - new_peak)
        expo = jnp.exp(scores - new_peak[:, :, None])
        totals = totals * correction + jnp.sum(expo, axis=-1)
        mixed = jnp.einsum(
            "hqk,khd->hqd",
            expo.astype(jnp.bfloat16),
            value_block,
            preferred_element_type=jnp.float32,
        )
        accum = accum * correction[:, :, None] + mixed
        return ((new_peak, totals, accum), None)

    def fold(carry, piece, start):
        keys, values = piece
        count = keys.shape[0]
        block = block_size(count)
        key_blocks = keys.reshape(count // block, block, heads, HEAD_DIM)
        value_blocks = values.reshape(count // block, block, heads, HEAD_DIM)
        result, unused = lax.scan(update, carry, (key_blocks, value_blocks))
        return result

    start_state = (
        jnp.full((heads, rows), -1e30, jnp.float32),
        jnp.zeros((heads, rows), jnp.float32),
        jnp.zeros((heads, rows, HEAD_DIM), jnp.float32),
    )
    return (fold, start_state)


def finish(state):
    peak, totals, accum = state
    heads, rows = totals.shape
    output = (accum / totals[:, :, None]).astype(jnp.bfloat16)
    return output.transpose(1, 0, 2).reshape(rows, heads * HEAD_DIM)


def make_hint(patches, hint_weight):
    normed = normalize_rows(patches, jnp.float32(1.0))
    return jnp.dot(normed, hint_weight, preferred_element_type=jnp.float32).astype(jnp.bfloat16)


def shards(
    query_proj,
    key_proj,
    value_proj,
    query_gain,
    key_gain,
    control,
    hint_weight,
    hint_gain,
    owner_map,
    layer_index,
):
    query_normed = normalize_rows(query_proj, query_gain)
    key_normed = normalize_rows(key_proj, key_gain)
    query_heads, key_heads, value_heads = (
        lax.all_to_all(query_normed, "ulysses", split_axis=1, concat_axis=0, tiled=True),
        lax.all_to_all(key_normed, "ulysses", split_axis=1, concat_axis=0, tiled=True),
        lax.all_to_all(value_proj, "ulysses", split_axis=1, concat_axis=0, tiled=True),
    )
    fold, start_state = make_fold(query_heads)
    state = fold(
        start_state,
        (
            lax.all_gather(key_heads, "blk", axis=0, tiled=True),
            lax.all_gather(value_heads, "blk", axis=0, tiled=True),
        ),
        jnp.int32(0),
    )
    attended = lax.all_to_all(finish(state), "ulysses", split_axis=0, concat_axis=1, tiled=True)
    owners = lax.axis_size("ulysses")
    tok_rows = control.shape[0]
    slab_rows = tok_rows // owners
    positions = jnp.arange(owners, dtype=jnp.int32)
    match = (owner_map[0][:, None] == positions[None, :]).astype(jnp.int32)
    inverse = jnp.sum(positions[:, None] * match, axis=0)
    gain_row = lax.dynamic_index_in_dim(hint_gain, layer_index[0], 0, keepdims=False)
    outgoing = jnp.take(control.reshape(owners, slab_rows, control.shape[1]), inverse, axis=0)
    arrived = lax.all_to_all(outgoing, "ulysses", split_axis=0, concat_axis=0, tiled=True).reshape(
        tok_rows, control.shape[1]
    )
    placed = make_hint(arrived, hint_weight)
    return (attended.astype(jnp.float32) + placed.astype(jnp.float32) * gain_row).astype(
        jnp.bfloat16
    )


def solution(mesh):
    return jax.shard_map(
        shards,
        mesh=mesh,
        in_specs=(
            P(("groups", "blk", "ulysses"), None),
            P(("groups", "blk", "ulysses"), None),
            P(("groups", "blk", "ulysses"), None),
            P(),
            P(),
            P(("groups", "blk", "ulysses"), None),
            P(),
            P(),
            P(("groups", "blk", "ulysses"), None),
            P(("groups", "blk", "ulysses")),
        ),
        out_specs=P(("groups", "blk", "ulysses"), None),
        check_vma=False,
    )
```

profile of v0, /device:TPU:0, one launch (start us, length us, event | category | flops | bytes accessed | tf_op | source)
XLA Modules:
  0.0 61.8 jit_solution(5780773453348342455)
XLA Ops:
  0.0 0.0 copy-start
  0.0 0.0 copy-start.6
  0.0 0.7 %copy-done.6 = s32[1,4]{1,0:T(1,128)S(1)} copy-done((s32[1,4]{1,0:T(1,128)S(1)}, s32[1,4]{1,0:T(1,128)}, u32[]{:S(2)}) %copy-start.6) | copy-done | bytes 40
  0.7 0.1 select_reduce_fusion
  0.8 0.0 copy-start.1
  0.9 1.3 %gather_fusion = bf16[4,8,384]{2,1,0:T(8,128)(2,1)S(1)} fusion(bf16[4,8,384]{2,1,0:T(8,128)(2,1)} %bitcast.69, s32[1024]{0:T(1024)S(1)} %pad_clamp_fusion), kind=kCustom, calls=%fused_computation | custom fusion | bytes 49168 | tf_op jit(solution)/shard_map/jit(_take)/gather | solution.py:113
  2.2 0.7 %broadcast_select_fusion = bf16[4,8,384]{2,1,0:T(8,128)(2,1)} fusion(bf16[4,8,384]{2,1,0:T(8,128)(2,1)S(1)} %gather_fusion, pred[4]{0:T(512)(128)(4,1)S(1)} %compare_and_fusion), kind=kLoop, calls=%fused_computation.36 | loop fusion | flops 12288 | bytes 49156 | tf_op jit(solution)/shard_map/jit(_take)/select_n | solution.py:113
  2.9 0.0 copy-start.2
  2.9 6.5 %all-to-all-start.4 = ((bf16[4,8,384]{2,1,0:T(8,128)(2,1)}), bf16[4,8,384]{2,1,0:T(8,128)(2,1)S(1)}, u32[]{:S(2)}, u32[]{:S(2)}) async-start(bf16[4,8,384]{2,1,0:T(8,128)(2,1)} %broadcast_select_fusion), calls=%async_computation.4 | async-start | bytes 49152 | tf_op jit(solution)/shard_map/all_to_all | solution.py:114
  9.3 0.0 copy-done.1
  9.3 0.1 fusion.14
  9.5 0.0 copy-done.2
  9.5 0.0 copy-start.4
  9.5 0.1 fusion.11
  10.3 0.0 copy-done.4
  10.3 0.0 copy-start.5
  10.3 0.1 fusion.16
  10.4 0.6 copy-done.5
  11.0 0.1 fusion.13
  11.1 0.8 %constant_dynamic-slice_fusion = f32[1,1024]{1,0:T(1,128)S(1)} fusion(f32[8,1024]{1,0:T(8,128)} %param.17, s32[]{:T(128)S(6)} %select_n.27), kind=kLoop, calls=%fused_computation.50 | loop fusion | bytes 8196 | tf_op jit(solution)/shard_map/jit(dynamic_index_in_dim)/dynamic_slice | solution.py:112
  11.9 0.6 copy.63
  12.5 0.0 copy-start.3
  12.5 0.6 %copy.64 = bf16[4,4,8,256]{3,2,0,1:T(8,128)(2,1)} copy(bf16[4,4,8,256]{3,2,1,0:T(8,128)(2,1)S(1)} %bitcast.67) | data formatting | bytes 131072 | tf_op jit(solution)/shard_map/all_to_all | solution.py:92
  13.1 0.2 copy-done.3
  13.3 0.6 %copy.62 = bf16[4,4,8,256]{3,2,0,1:T(8,128)(2,1)} copy(bf16[4,4,8,256]{3,2,1,0:T(8,128)(2,1)S(1)} %bitcast.68) | data formatting | bytes 131072 | tf_op jit(solution)/shard_map/all_to_all | solution.py:94
  14.0 1.0 %all-to-all-done.4 = bf16[4,8,384]{2,1,0:T(8,128)(2,1)S(1)} async-done(((bf16[4,8,384]{2,1,0:T(8,128)(2,1)}), bf16[4,8,384]{2,1,0:T(8,128)(2,1)S(1)}, u32[]{:S(2)}, u32[]{:S(2)}) %all-to-all-start.4) | async-done | bytes 24608 | tf_op jit(solution)/shard_map/all_to_all | solution.py:114
  15.0 4.1 %all-to-all-start.1 = ((bf16[32,4,256]{2,0,1:T(8,128)(2,1)}), bf16[32,4,256]{2,0,1:T(8,128)(2,1)S(1)}, u32[]{:S(2)}, u32[]{:S(2)}) async-start(bf16[32,4,256]{2,0,1:T(8,128)(2,1)} %bitcast.55), calls=%async_computation.1 | async-start | bytes 131072 | tf_op jit(solution)/shard_map/all_to_all | solution.py:93
  19.1 0.1 fusion.20
  19.2 5.7 %all-to-all-done.1 = bf16[32,4,256]{2,0,1:T(8,128)(2,1)S(1)} async-done(((bf16[32,4,256]{2,0,1:T(8,128)(2,1)}), bf16[32,4,256]{2,0,1:T(8,128)(2,1)S(1)}, u32[]{:S(2)}, u32[]{:S(2)}) %all-to-all-start.1) | async-done | bytes 65568 | tf_op jit(solution)/shard_map/all_to_all | solution.py:93
  24.8 3.3 %all-to-all-start = ((bf16[32,4,256]{2,0,1:T(8,128)(2,1)}), bf16[32,4,256]{2,0,1:T(8,128)(2,1)S(1)}, u32[]{:S(2)}, u32[]{:S(2)}) async-start(bf16[32,4,256]{2,0,1:T(8,128)(2,1)} %bitcast.56), calls=%async_computation | async-start | bytes 131072 | tf_op jit(solution)/shard_map/all_to_all | solution.py:92
  28.1 5.8 %all_gather.6 = bf16[512,256]{1,0:T(8,128)(2,1)S(1)} all-gather(bf16[128,256]{1,0:T(8,128)(2,1)S(1)} %bitcast.63), channel_id=1, replica_groups=mesh['groups'=2,'blk'=4,'ulysses'=4] {'blk'}, dimensions={0}, use_global_device_ids=true | all-gather | bytes 327680 | tf_op jit(solution)/shard_map/all_gather | solution.py:100
  33.9 0.1 copy.41
  34.0 0.0 all-to-all-done
  34.0 5.1 %all-to-all-start.2 = ((bf16[32,4,256]{2,0,1:T(8,128)(2,1)}), bf16[32,4,256]{2,0,1:T(8,128)(2,1)S(1)}, u32[]{:S(2)}, u32[]{:S(2)}) async-start(bf16[32,4,256]{2,0,1:T(8,128)(2,1)} %bitcast.54), calls=%async_computation.2 | async-start | bytes 131072 | tf_op jit(solution)/shard_map/all_to_all | solution.py:94
  39.1 0.3 fusion.24
  39.4 0.2 fusion.7
  39.7 5.2 %all-to-all-done.2 = bf16[32,4,256]{2,0,1:T(8,128)(2,1)S(1)} async-done(((bf16[32,4,256]{2,0,1:T(8,128)(2,1)}), bf16[32,4,256]{2,0,1:T(8,128)(2,1)S(1)}, u32[]{:S(2)}, u32[]{:S(2)}) %all-to-all-start.2) | async-done | bytes 65568 | tf_op jit(solution)/shard_map/all_to_all | solution.py:94
  44.8 5.8 %all_gather.7 = bf16[512,256]{1,0:T(8,128)(2,1)S(1)} all-gather(bf16[128,256]{1,0:T(8,128)(2,1)S(1)} %bitcast.62), channel_id=1, replica_groups=mesh['groups'=2,'blk'=4,'ulysses'=4] {'blk'}, dimensions={0}, use_global_device_ids=true | all-gather | bytes 327680 | tf_op jit(solution)/shard_map/all_gather | solution.py:101
  50.6 0.1 copy.45
  50.7 0.3 fusion.2
  51.0 0.1 copy.47
  51.1 0.7 %all_to_all.64 = bf16[4,32,256]{2,1,0:T(8,128)(2,1)} reshape(bf16[128,2,128]{2,1,0:T(2,128)(2,1)S(1)} %copy.47) | data formatting | bytes 131072 | tf_op jit(solution)/shard_map/all_to_all | solution.py:105
  51.8 3.3 %all-to-all-start.3 = ((bf16[4,32,256]{2,1,0:T(8,128)(2,1)}), bf16[4,32,256]{2,1,0:T(8,128)(2,1)S(1)}, u32[]{:S(2)}, u32[]{:S(2)}) async-start(bf16[4,32,256]{2,1,0:T(8,128)(2,1)} %all_to_all.64), calls=%async_computation.3 | async-start | bytes 131072 | tf_op jit(solution)/shard_map/all_to_all | solution.py:105
  55.1 0.1 rsqrt.30
  55.2 5.6 %all-to-all-done.3 = bf16[4,32,256]{2,1,0:T(8,128)(2,1)S(1)} async-done(((bf16[4,32,256]{2,1,0:T(8,128)(2,1)}), bf16[4,32,256]{2,1,0:T(8,128)(2,1)S(1)}, u32[]{:S(2)}, u32[]{:S(2)}) %all-to-all-start.3) | async-done | bytes 65568 | tf_op jit(solution)/shard_map/all_to_all | solution.py:105
  60.8 0.0 copy-done
  60.8 0.9 %fusion.6 = bf16[32,1024]{1,0:T(8,128)(2,1)} fusion(f32[32,1024]{1,0:T(8,128)S(1)} %bitcast.61, bf16[384,1024]{1,0:T(8,128)(2,1)S(1)} %copy-done, f32[1024]{0:T(1024)S(1)} %bitcast.70, bf16[4,8,384]{2,1,0:T(8,128)(2,1)S(1)} %all-to-all-done.4, f32[32]{0:T(128)S(1)} %rsqrt.30), kind=kOutput, calls=%fused_computation.10 | convolution fusion | flops 25366528 | bytes 1011840 | tf_op jit(solution)/shard_map/dot_general | solution.py:74
  (11 shorter events, 0.1 us)
Async XLA Ops:
  0.0 60.8 %copy-start = (bf16[384,1024]{1,0:T(8,128)(2,1)S(1)}, bf16[384,1024]{1,0:T(8,128)(2,1)}, u32[]{:S(2)}) copy-start(bf16[384,1024]{1,0:T(8,128)(2,1)} %param.16) | copy-start | bytes 2359300
  0.0 0.7 %copy-start.6 = (s32[1,4]{1,0:T(1,128)S(1)}, s32[1,4]{1,0:T(1,128)}, u32[]{:S(2)}) copy-start(s32[1,4]{1,0:T(1,128)} %param.18) | copy-start | bytes 52
  0.8 8.5 %copy-start.1 = (bf16[32,1024]{1,0:T(8,128)(2,1)S(1)}, bf16[32,1024]{1,0:T(8,128)(2,1)}, u32[]{:S(2)}) copy-start(bf16[32,1024]{1,0:T(8,128)(2,1)} %param.11) | copy-start | bytes 196612
  2.9 6.6 %copy-start.2 = (bf16[32,1024]{1,0:T(8,128)(2,1)S(1)}, bf16[32,1024]{1,0:T(8,128)(2,1)}, u32[]{:S(2)}) copy-start(bf16[32,1024]{1,0:T(8,128)(2,1)} %param.10) | copy-start | bytes 196612
  2.9 12.1 %all-to-all-start.4 = ((bf16[4,8,384]{2,1,0:T(8,128)(2,1)}), bf16[4,8,384]{2,1,0:T(8,128)(2,1)S(1)}, u32[]{:S(2)}, u32[]{:S(2)}) async-start(bf16[4,8,384]{2,1,0:T(8,128)(2,1)} %broadcast_select_fusion), calls=%async_computation.4 | async-start | bytes 49152 | tf_op jit(solution)/shard_map/all_to_all | solution.py:114
  9.5 0.8 %copy-start.4 = (f32[1024]{0:T(1024)S(1)}, f32[1024]{0:T(1024)}, u32[]{:S(2)}) copy-start(f32[1024]{0:T(1024)} %param.14) | copy-start | bytes 12292
  10.3 0.7 %copy-start.5 = (f32[1024]{0:T(1024)S(1)}, f32[1024]{0:T(1024)}, u32[]{:S(2)}) copy-start(f32[1024]{0:T(1024)} %param.13) | copy-start | bytes 12292
  12.5 0.9 %copy-start.3 = (bf16[32,1024]{1,0:T(8,128)(2,1)S(1)}, bf16[32,1024]{1,0:T(8,128)(2,1)}, u32[]{:S(2)}) copy-start(bf16[32,1024]{1,0:T(8,128)(2,1)} %param.12) | copy-start | bytes 196612
  15.0 9.8 %all-to-all-start.1 = ((bf16[32,4,256]{2,0,1:T(8,128)(2,1)}), bf16[32,4,256]{2,0,1:T(8,128)(2,1)S(1)}, u32[]{:S(2)}, u32[]{:S(2)}) async-start(bf16[32,4,256]{2,0,1:T(8,128)(2,1)} %bitcast.55), calls=%async_computation.1 | async-start | bytes 131072 | tf_op jit(solution)/shard_map/all_to_all | solution.py:93
  24.8 9.2 %all-to-all-start = ((bf16[32,4,256]{2,0,1:T(8,128)(2,1)}), bf16[32,4,256]{2,0,1:T(8,128)(2,1)S(1)}, u32[]{:S(2)}, u32[]{:S(2)}) async-start(bf16[32,4,256]{2,0,1:T(8,128)(2,1)} %bitcast.56), calls=%async_computation | async-start | bytes 131072 | tf_op jit(solution)/shard_map/all_to_all | solution.py:92
  34.0 10.8 %all-to-all-start.2 = ((bf16[32,4,256]{2,0,1:T(8,128)(2,1)}), bf16[32,4,256]{2,0,1:T(8,128)(2,1)S(1)}, u32[]{:S(2)}, u32[]{:S(2)}) async-start(bf16[32,4,256]{2,0,1:T(8,128)(2,1)} %bitcast.54), calls=%async_computation.2 | async-start | bytes 131072 | tf_op jit(solution)/shard_map/all_to_all | solution.py:94
  51.8 9.0 %all-to-all-start.3 = ((bf16[4,32,256]{2,1,0:T(8,128)(2,1)}), bf16[4,32,256]{2,1,0:T(8,128)(2,1)S(1)}, u32[]{:S(2)}, u32[]{:S(2)}) async-start(bf16[4,32,256]{2,1,0:T(8,128)(2,1)} %all_to_all.64), calls=%async_computation.3 | async-start | bytes 131072 | tf_op jit(solution)/shard_map/all_to_all | solution.py:105
where the time goes:
time: 62.6 us; the launch traced here: 61.8 us
  starting transfers between devices  22.2 us (35%)
  waiting for transfers between devices  17.5 us (28%)
  blocking collectives  11.5 us (18%)
  local copies, waits for them, and re-layouts  6.69 us (11%)
  other arithmetic  1.57 us (3%)
  matrix products  1.51 us (2%)
  between operations  0.82 us (1%)
    all_to_all x1, starting transfers between devices, shards(): lax.all_to_all(outgoing, 'ulysses', split_axis=0, concat_axis=0, tiled=True)  6.48 us
    all_gather x1, blocking collectives, shards(): lax.all_gather(key_heads, 'blk', axis=0, tiled=True)  5.78 us
    all_gather x1, blocking collectives, shards(): lax.all_gather(value_heads, 'blk', axis=0, tiled=True)  5.76 us
    all_to_all x1, waiting for transfers between devices, shards(): lax.all_to_all(key_normed, 'ulysses', split_axis=1, concat_axis=0, tiled=...  5.65 us
    all_to_all x1, waiting for transfers between devices, shards(): lax.all_to_all(finish(state), 'ulysses', split_axis=0, concat_axis=1, til...  5.61 us
    all_to_all x1, waiting for transfers between devices, shards(): lax.all_to_all(value_proj, 'ulysses', split_axis=1, concat_axis=0, tiled=...  5.17 us
    all_to_all x1, starting transfers between devices, shards(): lax.all_to_all(value_proj, 'ulysses', split_axis=1, concat_axis=0, tiled=...  5.05 us
    all_to_all x1, starting transfers between devices, shards(): lax.all_to_all(key_normed, 'ulysses', split_axis=1, concat_axis=0, tiled=...  4.08 us
  transfers between devices with their start and end apart: 5, of which 4 were waited for; matrix products, arithmetic and copies ran while one was open for 6% of the time, Pallas kernels for 0%

commit v1 on v0

--- a/solution.py
+++ b/solution.py
@@ -1,9 +1,16 @@
+import functools
+import math
+
 import jax
 import jax.numpy as jnp
 from jax import lax
+from jax.experimental import pallas as pl
+from jax.experimental.pallas import tpu as pltpu
 from jax.sharding import PartitionSpec as P
 
 HEAD_DIM = 128
+CORES = 2
+MESH = pl.DeviceIdType.MESH
 
 
 def normalize_rows(rows, gain):
@@ -120,9 +127,319 @@
     )
 
 
+def row_scale(values):
+    return lax.rsqrt(jnp.mean(values * values, axis=-1, keepdims=True) + 1e-06)
+
+
+def kernel(
+    blks,
+    owners,
+    query_hbm,
+    key_hbm,
+    value_hbm,
+    query_gain_hbm,
+    key_gain_hbm,
+    control_hbm,
+    weight_hbm,
+    gain_hbm,
+    owner_smem,
+    layer_smem,
+    out_ref,
+    query_in,
+    key_in,
+    value_in,
+    query_gain,
+    key_gain,
+    control_in,
+    weight,
+    gains,
+    stage,
+    landed,
+    passed,
+    slabs_out,
+    slabs_in,
+    mixed_out,
+    attended,
+    hint,
+    load_sem,
+    send_sem,
+    recv_sem,
+    pass_send,
+    pass_recv,
+    slab_send,
+    slab_recv,
+    back_send,
+    back_recv,
+):
+    rows = query_in.shape[0]
+    cols = blks // CORES
+    chips = cols * owners
+    slab_rows = rows // owners
+    b = lax.axis_index("blk")
+    u = lax.axis_index("ulysses")
+    parity = lax.rem(b, CORES)
+    x = b // CORES
+    me = x * owners + u
+    partner = {"blk": x * CORES + (1 - parity)}
+
+    loads = [
+        pltpu.make_async_copy(source, target, load_sem.at[at])
+        for at, (source, target) in enumerate(
+            (
+                (query_hbm, query_in),
+                (query_gain_hbm, query_gain),
+                (key_hbm, key_in),
+                (key_gain_hbm, key_gain),
+                (value_hbm, value_in),
+                (control_hbm, control_in),
+                (weight_hbm, weight),
+                (gain_hbm, gains),
+            )
+        )
+    ]
+    for load in loads:
+        load.start()
+
+    others = []
+    for dz in sorted(range(owners), key=lambda d: -min(d, owners - d)):
+        for dx in reversed(range(cols)):
+            if dx or dz:
+                there_x = lax.rem(x + dx, cols)
+                there_u = lax.rem(u + dz, owners)
+                others.append(
+                    (
+                        there_x * owners + there_u,
+                        {"blk": there_x * CORES + parity, "ulysses": there_u},
+                    )
+                )
+
+    barrier = pltpu.get_barrier_semaphore()
+    for _, device in others:
+        pl.semaphore_signal(barrier, inc=1, device_id=device, device_id_type=MESH)
+    pl.semaphore_signal(barrier, inc=1, device_id=partner, device_id_type=MESH)
+
+    for first, gain, part in ((query_in, query_gain, 0), (key_in, key_gain, 1)):
+        loads[2 * part].wait()
+        loads[2 * part + 1].wait()
+        values = first[...].astype(jnp.float32)
+        normed = (values * row_scale(values) * gain[...]).astype(jnp.bfloat16)
+        for h in range(chips):
+            stage[h, part * rows : (part + 1) * rows] = normed[
+                :, h * HEAD_DIM : (h + 1) * HEAD_DIM
+            ]
+    loads[4].wait()
+    for h in range(chips):
+        stage[h, 2 * rows :] = value_in[:, h * HEAD_DIM : (h + 1) * HEAD_DIM]
+
+    loads[5].wait()
+    values = control_in[...].astype(jnp.float32)
+    normed = values * row_scale(values)
+    pieces = [normed[j * slab_rows : (j + 1) * slab_rows] for j in range(owners)]
+    for to in range(owners):
+        picked = pieces[0]
+        for j in range(1, owners):
+            picked = jnp.where(owner_smem[0, j] == to, pieces[j], picked)
+        slabs_out[to] = picked.astype(jnp.bfloat16)
+
+    pl.semaphore_wait(barrier, len(others) + 1)
+
+    started = []
+
+    def send(source, target, sem_out, sem_in, device):
+        copy = pltpu.make_async_remote_copy(
+            src_ref=source,
+            dst_ref=target,
+            send_sem=sem_out,
+            recv_sem=sem_in,
+            device_id=device,
+            device_id_type=MESH,
+        )
+        copy.start()
+        started.append(copy)
+
+    def arrive(target, sem_out, sem_in):
+        pltpu.make_async_remote_copy(
+            src_ref=target,
+            dst_ref=target,
+            send_sem=sem_out,
+            recv_sem=sem_in,
+            device_id=partner,
+            device_id_type=MESH,
+        ).wait_recv()
+
+    for at, (there, device) in enumerate(others):
+        send(stage.at[there], landed.at[me], send_sem.at[at], recv_sem.at[me], device)
+    send(
+        stage.at[me, pl.ds(rows, 2 * rows)],
+        passed.at[me],
+        pass_send.at[me],
+        pass_recv.at[me],
+        partner,
+    )
+    for d in range(1, owners):
+        there = lax.rem(u + d, owners)
+        send(
+            slabs_out.at[there],
+            slabs_in.at[u],
+            slab_send.at[d],
+            slab_recv.at[u],
+            {"ulysses": there},
+        )
+    landed[me] = stage[me]
+    slabs_in[u] = slabs_out[u]
+
+    loads[6].wait()
+    loads[7].wait()
+    for d in range(1, owners):
+        source = lax.rem(u + owners - d, owners)
+        arrive(slabs_in.at[source], slab_send.at[0], slab_recv.at[source])
+    arrived = slabs_in[...].astype(jnp.float32).reshape(rows, control_in.shape[1])
+    placed = jnp.dot(
+        arrived.astype(jnp.bfloat16), weight[...], preferred_element_type=jnp.float32
+    ).astype(jnp.bfloat16)
+    hint[...] = placed.astype(jnp.float32) * gains[pl.ds(layer_smem[0], 1), :]
+
+    for there, _ in reversed(others):
+        arrive(landed.at[there], pass_send.at[0], recv_sem.at[there])
+        send(
+            landed.at[there, pl.ds(rows, 2 * rows)],
+            passed.at[there],
+            pass_send.at[there],
+            pass_recv.at[there],
+            partner,
+        )
+    for there in [me] + [t for t, _ in reversed(others)]:
+        arrive(passed.at[there], pass_send.at[0], pass_recv.at[there])
+
+    count = chips * rows
+    keys = jnp.concatenate(
+        [
+            landed[:, rows : 2 * rows].reshape(count, HEAD_DIM),
+            passed[:, :rows].reshape(count, HEAD_DIM),
+        ],
+        axis=0,
+    )
+    mix = jnp.concatenate(
+        [
+            landed[:, 2 * rows :].reshape(count, HEAD_DIM),
+            passed[:, rows:].reshape(count, HEAD_DIM),
+        ],
+        axis=0,
+    )
+    factor = HEAD_DIM ** (-0.5) * math.log2(math.e)
+    targets = others + [(me, None)]
+    group = max(1, chips // GROUPS)
+    waiting = []
+
+    def flush():
+        for there, device, at in waiting:
+            send(
+                mixed_out.at[there],
+                attended.at[me],
+                back_send.at[at],
+                back_recv.at[me],
+                device,
+            )
+        waiting.clear()
+
+    for base in range(0, chips, group):
+        part = targets[base : base + group]
+        queries = jnp.concatenate([landed[there, :rows] for there, _ in part], axis=0)
+        scores = lax.dot_general(
+            queries, keys, (((1,), (1,)), ((), ())), preferred_element_type=jnp.float32
+        )
+        peak = jnp.max(scores, axis=-1, keepdims=True)
+        expo = jnp.exp2((scores - peak) * factor)
+        totals = jnp.sum(expo, axis=-1, keepdims=True)
+        output = jnp.dot(
+            expo.astype(jnp.bfloat16), mix, preferred_element_type=jnp.float32
+        )
+        output = (output * (1.0 / totals)).astype(jnp.bfloat16)
+        flush()
+        for at, (there, device) in enumerate(part):
+            piece = output[at * rows : (at + 1) * rows]
+            if device is None:
+                attended[there] = piece
+            else:
+                mixed_out[there] = piece
+                waiting.append((there, device, base + at))
+    flush()
+
+    for there, _ in reversed(others):
+        arrive(attended.at[there], back_send.at[0], back_recv.at[there])
+    for h in range(chips):
+        columns = slice(h * HEAD_DIM, (h + 1) * HEAD_DIM)
+        out_ref[:, columns] = (attended[h].astype(jnp.float32) + hint[:, columns]).astype(
+            jnp.bfloat16
+        )
+    for copy in started:
+        copy.wait_send()
+
+
+GROUPS = 2
+
+
+def run(blks, owners, *arrays):
+    query_proj, control, hint_weight, hint_gain = arrays[0], arrays[5], arrays[6], arrays[7]
+    rows, feats = query_proj.shape
+    chips = blks // CORES * owners
+    fits = (
+        blks % CORES == 0
+        and chips * HEAD_DIM == feats
+        and rows % 16 == 0
+        and rows % owners == 0
+        and (rows // owners) % 8 == 0
+        and rows * chips <= 1024
+    )
+    if not fits:
+        return shards(*arrays)
+    inner = control.shape[1]
+    dma = pltpu.SemaphoreType.DMA
+    half = jnp.bfloat16
+    wide = jnp.float32
+    operands = list(arrays)
+    operands[3] = arrays[3].reshape(1, feats)
+    operands[4] = arrays[4].reshape(1, feats)
+    return pl.pallas_call(
+        functools.partial(kernel, blks, owners),
+        out_shape=jax.ShapeDtypeStruct((rows, feats), half),
+        in_specs=[pl.BlockSpec(memory_space=pl.ANY)] * 8
+        + [pl.BlockSpec(memory_space=pltpu.SMEM)] * 2,
+        out_specs=pl.BlockSpec(memory_space=pltpu.VMEM),
+        scratch_shapes=[
+            pltpu.VMEM((rows, feats), half),
+            pltpu.VMEM((rows, feats), half),
+            pltpu.VMEM((rows, feats), half),
+            pltpu.VMEM((1, feats), wide),
+            pltpu.VMEM((1, feats), wide),
+            pltpu.VMEM((rows, inner), half),
+            pltpu.VMEM(hint_weight.shape, half),
+            pltpu.VMEM(hint_gain.shape, wide),
+            pltpu.VMEM((chips, 3 * rows, HEAD_DIM), half),
+            pltpu.VMEM((chips, 3 * rows, HEAD_DIM), half),
+            pltpu.VMEM((chips, 2 * rows, HEAD_DIM), half),
+            pltpu.VMEM((owners, rows // owners, inner), half),
+            pltpu.VMEM((owners, rows // owners, inner), half),
+            pltpu.VMEM((chips, rows, HEAD_DIM), half),
+            pltpu.VMEM((chips, rows, HEAD_DIM), half),
+            pltpu.VMEM((rows, feats), wide),
+            dma((8,)),
+            dma((chips,)),
+            dma((chips,)),
+            dma((chips,)),
+            dma((chips,)),
+            dma((owners,)),
+            dma((owners,)),
+            dma((chips,)),
+            dma((chips,)),
+        ],
+        compiler_params=pltpu.CompilerParams(collective_id=0, has_side_effects=True),
+    )(*operands)
+
+
 def solution(mesh):
     return jax.shard_map(
-        shards,
+        functools.partial(run, mesh.shape["blk"], mesh.shape["ulysses"]),
         mesh=mesh,
         in_specs=(
             P(("groups", "blk", "ulysses"), None),

time: 62.6 us -> 21.2 us (0.34)
  starting transfers between devices: 22.2 us -> 0 us
  Pallas kernels: 0 us -> 18.8 us
  waiting for transfers between devices: 17.5 us -> 0 us
  blocking collectives: 11.5 us -> 0 us
  local copies, waits for them, and re-layouts: 6.69 us -> 1.47 us
  other arithmetic: 1.57 us -> 0 us
  matrix products: 1.51 us -> 0 us
    all_to_all x5 -> x0, starting transfers between devices: 22.2 us -> none  [the longest x1 6.48 us: shards(): lax.all_to_all(outgoing, 'ulysses', split_axis=0, concat_axis=0, tiled=True)]
    pallas_call x0 -> x1, Pallas kernels: none -> 18.8 us  [run(): pl.pallas_call(functools.partial(kernel, blks, owners), out_shape=jax.Sha...]
    all_to_all x5 -> x0, waiting for transfers between devices: 17.5 us -> none  [the longest x1 5.65 us: shards(): lax.all_to_all(key_normed, 'ulysses', split_axis=1, concat_axis=0, tiled=...]
    all_gather x2 -> x0, blocking collectives: 11.5 us -> none  [the longest x1 5.78 us: shards(): lax.all_gather(key_heads, 'blk', axis=0, tiled=True)]
    all_to_all x4 -> x0, local copies, waits for them, and re-layouts: 2.55 us -> none  [the longest x1 0.68 us: shards(): lax.all_to_all(finish(state), 'ulysses', split_axis=0, concat_axis=1, til...]
    dot_general x3 -> x0, matrix products: 1.51 us -> none  [the longest x1 0.93 us: make_hint(): jnp.dot(normed, hint_weight, preferred_element_type=jnp.float32)]
    gather x1 -> x0, local copies, waits for them, and re-layouts: 1.33 us -> none  [shards(): jnp.take(control.reshape(owners, slab_rows, control.shape[1]), inverse, a...]
    dynamic_slice x1 -> x0, local copies, waits for them, and re-layouts: 0.77 us -> none  [shards(): lax.dynamic_index_in_dim(hint_gain, layer_index[0], 0, keepdims=False)]
  transfers between devices with their start and end apart: 5 -> 0, of which waited for: 4 -> 0; matrix products, arithmetic and copies ran while one was open for 6% -> 0% of each run, Pallas kernels for 0% -> 0%
where the time goes in v1:
time: 21.2 us; the launch traced here: 21 us
  Pallas kernels  18.8 us (89%)
  local copies, waits for them, and re-layouts  1.47 us (7%)
  between operations  0.66 us (3%)
    pallas_call x1, Pallas kernels, run(): pl.pallas_call(functools.partial(kernel, blks, owners), out_shape=jax.Sha...  18.8 us
    unnamed x1, local copies, waits for them, and re-layouts  1.47 us

profile of v1, /device:TPU:0, one launch (start us, length us, event | category | flops | bytes accessed | tf_op | source)
XLA Modules:
  0.0 21.0 jit_solution(142378700720207034)
XLA Ops:
  0.7 18.8 %shard_map.100 = bf16[32,1024]{1,0:T(8,128)(2,1)} custom-call(bf16[32,1024]{1,0:T(8,128)(2,1)} %query_hbm.1, bf16[32,1024]{1,0:T(8,128)(2,1)} %key_hbm.1, bf16[32,1024]{1,0:T(8,128)(2,1)} %value_hbm.1, f32[1,1024]{1,0:T(1,128)} %bitcast.2, f32[1,1024]{1,0:T(1,128)} %bitcast.3, bf16[32,384]{1,0:T(8,128)(2,1)} %control_hbm.1, bf16[384,1024]{1,0:T(8,128)(2,1)} %weight_hbm.1, ...), custom_call_target="tpu_custom_call" | custom-call | tf_op jit(solution)/shard_map/pallas_call | solution.py:403
  19.5 1.5 %copy.13 = bf16[32,1024]{1,0:T(8,128)(2,1)} copy(bf16[32,1024]{1,0:T(8,128)(2,1)} %shard_map.100) | data formatting | bytes 131072

commit v2 on v1

--- a/solution.py
+++ b/solution.py
@@ -142,7 +142,7 @@
     control_hbm,
     weight_hbm,
     gain_hbm,
-    owner_smem,
+    owner_hbm,
     layer_smem,
     out_ref,
     query_in,
@@ -153,6 +153,7 @@
     control_in,
     weight,
     gains,
+    owner_smem,
     stage,
     landed,
     passed,
@@ -194,6 +195,7 @@
                 (control_hbm, control_in),
                 (weight_hbm, weight),
                 (gain_hbm, gains),
+                (owner_hbm, owner_smem),
             )
         )
     ]
@@ -232,6 +234,7 @@
         stage[h, 2 * rows :] = value_in[:, h * HEAD_DIM : (h + 1) * HEAD_DIM]
 
     loads[5].wait()
+    loads[8].wait()
     values = control_in[...].astype(jnp.float32)
     normed = values * row_scale(values)
     pieces = [normed[j * slab_rows : (j + 1) * slab_rows] for j in range(owners)]
@@ -400,11 +403,13 @@
     operands = list(arrays)
     operands[3] = arrays[3].reshape(1, feats)
     operands[4] = arrays[4].reshape(1, feats)
+    layer = operands.pop()
+    operands = [pltpu.with_memory_space_constraint(array, pltpu.HBM) for array in operands]
     return pl.pallas_call(
         functools.partial(kernel, blks, owners),
         out_shape=jax.ShapeDtypeStruct((rows, feats), half),
-        in_specs=[pl.BlockSpec(memory_space=pl.ANY)] * 8
-        + [pl.BlockSpec(memory_space=pltpu.SMEM)] * 2,
+        in_specs=[pl.BlockSpec(memory_space=pltpu.HBM)] * len(operands)
+        + [pl.BlockSpec(memory_space=pltpu.SMEM)],
         out_specs=pl.BlockSpec(memory_space=pltpu.VMEM),
         scratch_shapes=[
             pltpu.VMEM((rows, feats), half),
@@ -415,6 +420,7 @@
             pltpu.VMEM((rows, inner), half),
             pltpu.VMEM(hint_weight.shape, half),
             pltpu.VMEM(hint_gain.shape, wide),
+            pltpu.SMEM((1, owners), jnp.int32),
             pltpu.VMEM((chips, 3 * rows, HEAD_DIM), half),
             pltpu.VMEM((chips, 3 * rows, HEAD_DIM), half),
             pltpu.VMEM((chips, 2 * rows, HEAD_DIM), half),
@@ -423,7 +429,7 @@
             pltpu.VMEM((chips, rows, HEAD_DIM), half),
             pltpu.VMEM((chips, rows, HEAD_DIM), half),
             pltpu.VMEM((rows, feats), wide),
-            dma((8,)),
+            dma((len(operands),)),
             dma((chips,)),
             dma((chips,)),
             dma((chips,)),
@@ -433,8 +439,10 @@
             dma((chips,)),
             dma((chips,)),
         ],
-        compiler_params=pltpu.CompilerParams(collective_id=0, has_side_effects=True),
-    )(*operands)
+        compiler_params=pltpu.CompilerParams(
+            collective_id=0, has_side_effects=True, vmem_limit_bytes=16 << 20
+        ),
+    )(*operands, layer)
 
 
 def solution(mesh):

time: 21.2 us -> 19 us (0.90)
  Pallas kernels: 18.8 us -> 17.6 us
  local copies, waits for them, and re-layouts: 1.47 us -> 0.63 us
    pallas_call x1, Pallas kernels: 18.8 us -> 17.6 us  [run(): pl.pallas_call(functools.partial(kernel, blks, owners), out_shape=jax.Sha...]
    unnamed x1, local copies, waits for them, and re-layouts: 1.47 us -> 0.63 us
where the time goes in v2:
time: 19 us; the launch traced here: 18.8 us
  Pallas kernels  17.6 us (93%)
  between operations  0.66 us (3%)
  local copies, waits for them, and re-layouts  0.63 us (3%)
    pallas_call x1, Pallas kernels, run(): pl.pallas_call(functools.partial(kernel, blks, owners), out_shape=jax.Sha...  17.6 us
    unnamed x1, local copies, waits for them, and re-layouts  0.63 us

profile of v2, /device:TPU:0, one launch (start us, length us, event | category | flops | bytes accessed | tf_op | source)
XLA Modules:
  0.0 18.8 jit_solution(712662521075170820)
XLA Ops:
  0.7 17.6 %shard_map.100 = bf16[32,1024]{1,0:T(8,128)(2,1)S(1)} custom-call(bf16[32,1024]{1,0:T(8,128)(2,1)} %query_hbm.1, bf16[32,1024]{1,0:T(8,128)(2,1)} %key_hbm.1, bf16[32,1024]{1,0:T(8,128)(2,1)} %value_hbm.1, f32[1,1024]{1,0:T(1,128)} %bitcast.2, f32[1,1024]{1,0:T(1,128)} %bitcast.3, bf16[32,384]{1,0:T(8,128)(2,1)} %control_hbm.1, ...), custom_call_target="tpu_custom_call" | custom-call | tf_op jit(solution)/shard_map/pallas_call | solution.py:408
  18.2 0.6 %copy.13 = bf16[32,1024]{1,0:T(8,128)(2,1)} copy(bf16[32,1024]{1,0:T(8,128)(2,1)S(1)} %shard_map.100) | data formatting | bytes 131072

commit v3 on v2

--- a/solution.py
+++ b/solution.py
@@ -171,6 +171,7 @@
     slab_recv,
     back_send,
     back_recv,
+    level_sem,
 ):
     rows = query_in.shape[0]
     cols = blks // CORES
@@ -215,10 +216,51 @@
                     )
                 )
 
+    around = (
+        (u > 0, {"ulysses": u - 1}),
+        (u < owners - 1, {"ulysses": u + 1}),
+        (x > 0, {"blk": b - CORES}),
+        (x < cols - 1, {"blk": b + CORES}),
+    )
+    near = (
+        (u + owners - 1) // owners
+        + (2 * owners - 2 - u) // owners
+        + (x + cols - 1) // cols
+        + (2 * cols - 2 - x) // cols
+    )
+
+    def tell(semaphore):
+        for inside, device in around:
+
+            @pl.when(inside)
+            def _():
+                pl.semaphore_signal(
+                    semaphore, inc=1, device_id=device, device_id_type=MESH
+                )
+
+    def ring(distance):
+        for dz in range(-distance, distance + 1):
+            for dx in sorted({abs(dz) - distance, distance - abs(dz)}):
+                if abs(dx) < cols and abs(dz) < owners:
+                    there_x, there_u = x + dx, u + dz
+                    inside = (
+                        (there_x >= 0)
+                        & (there_x < cols)
+                        & (there_u >= 0)
+                        & (there_u < owners)
+                    )
+                    yield inside, there_x * owners + there_u, {
+                        "blk": there_x * CORES + parity,
+                        "ulysses": there_u,
+                    }
+
+    farthest = cols + owners - 2
     barrier = pltpu.get_barrier_semaphore()
-    for _, device in others:
-        pl.semaphore_signal(barrier, inc=1, device_id=device, device_id_type=MESH)
+    tell(barrier)
     pl.semaphore_signal(barrier, inc=1, device_id=partner, device_id_type=MESH)
+    pl.semaphore_wait(barrier, near + 1)
+    if farthest > 1:
+        tell(level_sem.at[2])
 
     for first, gain, part in ((query_in, query_gain, 0), (key_in, key_gain, 1)):
         loads[2 * part].wait()
@@ -233,6 +275,53 @@
     for h in range(chips):
         stage[h, 2 * rows :] = value_in[:, h * HEAD_DIM : (h + 1) * HEAD_DIM]
 
+    started = []
+
+    def remote(source, target, sem_out, sem_in, device):
+        return pltpu.make_async_remote_copy(
+            src_ref=source,
+            dst_ref=target,
+            send_sem=sem_out,
+            recv_sem=sem_in,
+            device_id=device,
+            device_id_type=MESH,
+        )
+
+    def send(*way):
+        copy = remote(*way)
+        copy.start()
+        started.append(copy)
+
+    def arrive(target, sem_out, sem_in):
+        pltpu.make_async_remote_copy(
+            src_ref=target,
+            dst_ref=target,
+            send_sem=sem_out,
+            recv_sem=sem_in,
+            device_id=partner,
+            device_id_type=MESH,
+        ).wait_recv()
+
+    send(
+        stage.at[me, pl.ds(rows, 2 * rows)],
+        passed.at[me],
+        pass_send.at[me],
+        pass_recv.at[me],
+        partner,
+    )
+    for distance in range(1, farthest + 1):
+        if distance > 1:
+            pl.semaphore_wait(level_sem.at[distance], near)
+            if distance < farthest:
+                tell(level_sem.at[distance + 1])
+        for inside, there, device in ring(distance):
+
+            @pl.when(inside)
+            def _():
+                remote(
+                    stage.at[there], landed.at[me], send_sem.at[there], recv_sem.at[me], device
+                ).start()
+
     loads[5].wait()
     loads[8].wait()
     values = control_in[...].astype(jnp.float32)
@@ -244,41 +333,6 @@
             picked = jnp.where(owner_smem[0, j] == to, pieces[j], picked)
         slabs_out[to] = picked.astype(jnp.bfloat16)
 
-    pl.semaphore_wait(barrier, len(others) + 1)
-
-    started = []
-
-    def send(source, target, sem_out, sem_in, device):
-        copy = pltpu.make_async_remote_copy(
-            src_ref=source,
-            dst_ref=target,
-            send_sem=sem_out,
-            recv_sem=sem_in,
-            device_id=device,
-            device_id_type=MESH,
-        )
-        copy.start()
-        started.append(copy)
-
-    def arrive(target, sem_out, sem_in):
-        pltpu.make_async_remote_copy(
-            src_ref=target,
-            dst_ref=target,
-            send_sem=sem_out,
-            recv_sem=sem_in,
-            device_id=partner,
-            device_id_type=MESH,
-        ).wait_recv()
-
-    for at, (there, device) in enumerate(others):
-        send(stage.at[there], landed.at[me], send_sem.at[at], recv_sem.at[me], device)
-    send(
-        stage.at[me, pl.ds(rows, 2 * rows)],
-        passed.at[me],
-        pass_send.at[me],
-        pass_recv.at[me],
-        partner,
-    )
     for d in range(1, owners):
         there = lax.rem(u + d, owners)
         send(
@@ -290,6 +344,77 @@
         )
     landed[me] = stage[me]
     slabs_in[u] = slabs_out[u]
+
+    for distance in range(1, farthest + 1):
+        for inside, there, _ in ring(distance):
+
+            @pl.when(inside)
+            def _():
+                arrive(landed.at[there], pass_send.at[0], recv_sem.at[there])
+                remote(
+                    landed.at[there, pl.ds(rows, 2 * rows)],
+                    passed.at[there],
+                    pass_send.at[there],
+                    pass_recv.at[there],
+                    partner,
+                ).start()
+
+    for there in [me] + [t for t, _ in reversed(others)]:
+        arrive(passed.at[there], pass_send.at[0], pass_recv.at[there])
+
+    count = chips * rows
+    keys = jnp.concatenate(
+        [
+            landed[:, rows : 2 * rows].reshape(count, HEAD_DIM),
+            passed[:, :rows].reshape(count, HEAD_DIM),
+        ],
+        axis=0,
+    )
+    mix = jnp.concatenate(
+        [
+            landed[:, 2 * rows :].reshape(count, HEAD_DIM),
+            passed[:, rows:].reshape(count, HEAD_DIM),
+        ],
+        axis=0,
+    )
+    factor = HEAD_DIM ** (-0.5) * math.log2(math.e)
+    targets = others + [(me, None)]
+    group = max(1, chips // GROUPS)
+    waiting = []
+
+    def flush():
+        for there, device, at in waiting:
+            send(
+                mixed_out.at[there],
+                attended.at[me],
+                back_send.at[at],
+                back_recv.at[me],
+                device,
+            )
+        waiting.clear()
+
+    for base in range(0, chips, group):
+        part = targets[base : base + group]
+        queries = jnp.concatenate([landed[there, :rows] for there, _ in part], axis=0)
+        scores = lax.dot_general(
+            queries, keys, (((1,), (1,)), ((), ())), preferred_element_type=jnp.float32
+        )
+        peak = jnp.max(scores, axis=-1, keepdims=True)
+        expo = jnp.exp2((scores - peak) * factor)
+        totals = jnp.sum(expo, axis=-1, keepdims=True)
+        output = jnp.dot(
+            expo.astype(jnp.bfloat16), mix, preferred_element_type=jnp.float32
+        )
+        output = (output * (1.0 / totals)).astype(jnp.bfloat16)
+        flush()
+        for at, (there, device) in enumerate(part):
+            piece = output[at * rows : (at + 1) * rows]
+            if device is None:
+                attended[there] = piece
+            else:
+                mixed_out[there] = piece
+                waiting.append((there, device, base + at))
+    flush()
 
     loads[6].wait()
     loads[7].wait()
@@ -303,77 +428,24 @@
     hint[...] = placed.astype(jnp.float32) * gains[pl.ds(layer_smem[0], 1), :]
 
     for there, _ in reversed(others):
-        arrive(landed.at[there], pass_send.at[0], recv_sem.at[there])
-        send(
-            landed.at[there, pl.ds(rows, 2 * rows)],
-            passed.at[there],
-            pass_send.at[there],
-            pass_recv.at[there],
-            partner,
-        )
-    for there in [me] + [t for t, _ in reversed(others)]:
-        arrive(passed.at[there], pass_send.at[0], pass_recv.at[there])
-
-    count = chips * rows
-    keys = jnp.concatenate(
-        [
-            landed[:, rows : 2 * rows].reshape(count, HEAD_DIM),
-            passed[:, :rows].reshape(count, HEAD_DIM),
-        ],
-        axis=0,
-    )
-    mix = jnp.concatenate(
-        [
-            landed[:, 2 * rows :].reshape(count, HEAD_DIM),
-            passed[:, rows:].reshape(count, HEAD_DIM),
-        ],
-        axis=0,
-    )
-    factor = HEAD_DIM ** (-0.5) * math.log2(math.e)
-    targets = others + [(me, None)]
-    group = max(1, chips // GROUPS)
-    waiting = []
-
-    def flush():
-        for there, device, at in waiting:
-            send(
-                mixed_out.at[there],
-                attended.at[me],
-                back_send.at[at],
-                back_recv.at[me],
-                device,
-            )
-        waiting.clear()
-
-    for base in range(0, chips, group):
-        part = targets[base : base + group]
-        queries = jnp.concatenate([landed[there, :rows] for there, _ in part], axis=0)
-        scores = lax.dot_general(
-            queries, keys, (((1,), (1,)), ((), ())), preferred_element_type=jnp.float32
-        )
-        peak = jnp.max(scores, axis=-1, keepdims=True)
-        expo = jnp.exp2((scores - peak) * factor)
-        totals = jnp.sum(expo, axis=-1, keepdims=True)
-        output = jnp.dot(
-            expo.astype(jnp.bfloat16), mix, preferred_element_type=jnp.float32
-        )
-        output = (output * (1.0 / totals)).astype(jnp.bfloat16)
-        flush()
-        for at, (there, device) in enumerate(part):
-            piece = output[at * rows : (at + 1) * rows]
-            if device is None:
-                attended[there] = piece
-            else:
-                mixed_out[there] = piece
-                waiting.append((there, device, base + at))
-    flush()
-
-    for there, _ in reversed(others):
         arrive(attended.at[there], back_send.at[0], back_recv.at[there])
     for h in range(chips):
         columns = slice(h * HEAD_DIM, (h + 1) * HEAD_DIM)
         out_ref[:, columns] = (attended[h].astype(jnp.float32) + hint[:, columns]).astype(
             jnp.bfloat16
+        )
+    for there, device in others:
+        started.append(
+            remote(stage.at[there], landed.at[me], send_sem.at[there], recv_sem.at[me], device)
+        )
+        started.append(
+            remote(
+                landed.at[there, pl.ds(rows, 2 * rows)],
+                passed.at[there],
+                pass_send.at[there],
+                pass_recv.at[there],
+                partner,
+            )
         )
     for copy in started:
         copy.wait_send()
@@ -438,6 +510,7 @@
             dma((owners,)),
             dma((chips,)),
             dma((chips,)),
+            pltpu.SemaphoreType.REGULAR((blks // CORES + owners,)),
         ],
         compiler_params=pltpu.CompilerParams(
             collective_id=0, has_side_effects=True, vmem_limit_bytes=16 << 20

time: 19 us -> 18.8 us (0.989)
  Pallas kernels: 17.6 us -> 17.4 us
where the time goes in v3:
time: 18.8 us; the launch traced here: 18.7 us
  Pallas kernels  17.4 us (93%)
  between operations  0.66 us (4%)
  local copies, waits for them, and re-layouts  0.63 us (3%)
    pallas_call x1, Pallas kernels, run(): pl.pallas_call(functools.partial(kernel, blks, owners), out_shape=jax.Sha...  17.4 us
    unnamed x1, local copies, waits for them, and re-layouts  0.63 us

profile of v3, /device:TPU:0, one launch (start us, length us, event | category | flops | bytes accessed | tf_op | source)
XLA Modules:
  0.0 18.7 jit_solution(12617436138553223234)
XLA Ops:
  0.7 17.4 %shard_map.100 = bf16[32,1024]{1,0:T(8,128)(2,1)S(1)} custom-call(bf16[32,1024]{1,0:T(8,128)(2,1)} %query_hbm.1, bf16[32,1024]{1,0:T(8,128)(2,1)} %key_hbm.1, bf16[32,1024]{1,0:T(8,128)(2,1)} %value_hbm.1, f32[1,1024]{1,0:T(1,128)} %bitcast.2, f32[1,1024]{1,0:T(1,128)} %bitcast.3, bf16[32,384]{1,0:T(8,128)(2,1)} %control_hbm.1, ...), custom_call_target="tpu_custom_call" | custom-call | tf_op jit(solution)/shard_map/pallas_call | solution.py:480
  18.1 0.6 %copy.13 = bf16[32,1024]{1,0:T(8,128)(2,1)} copy(bf16[32,1024]{1,0:T(8,128)(2,1)S(1)} %shard_map.100) | data formatting | bytes 131072

commit v4 on v3

--- a/solution.py
+++ b/solution.py
@@ -156,7 +156,6 @@
     owner_smem,
     stage,
     landed,
-    passed,
     slabs_out,
     slabs_in,
     mixed_out,
@@ -165,8 +164,6 @@
     load_sem,
     send_sem,
     recv_sem,
-    pass_send,
-    pass_recv,
     slab_send,
     slab_recv,
     back_send,
@@ -174,15 +171,19 @@
     level_sem,
 ):
     rows = query_in.shape[0]
+    low, high = host_range(owners)
+    wide = high - low
+    heads = blks * wide
     cols = blks // CORES
-    chips = cols * owners
+    devices = blks * owners
     slab_rows = rows // owners
     b = lax.axis_index("blk")
     u = lax.axis_index("ulysses")
     parity = lax.rem(b, CORES)
     x = b // CORES
-    me = x * owners + u
-    partner = {"blk": x * CORES + (1 - parity)}
+    me = b * owners + u
+    own = b * wide + u - low
+    hosting = (u >= low) & (u < high)
 
     loads = [
         pltpu.make_async_copy(source, target, load_sem.at[at])
@@ -203,27 +204,16 @@
     for load in loads:
         load.start()
 
-    others = []
-    for dz in sorted(range(owners), key=lambda d: -min(d, owners - d)):
-        for dx in reversed(range(cols)):
-            if dx or dz:
-                there_x = lax.rem(x + dx, cols)
-                there_u = lax.rem(u + dz, owners)
-                others.append(
-                    (
-                        there_x * owners + there_u,
-                        {"blk": there_x * CORES + parity, "ulysses": there_u},
-                    )
-                )
-
     around = (
+        (b >= 0, {"blk": x * CORES + (1 - parity)}),
         (u > 0, {"ulysses": u - 1}),
         (u < owners - 1, {"ulysses": u + 1}),
         (x > 0, {"blk": b - CORES}),
         (x < cols - 1, {"blk": b + CORES}),
     )
     near = (
-        (u + owners - 1) // owners
+        1
+        + (u + owners - 1) // owners
         + (2 * owners - 2 - u) // owners
         + (x + cols - 1) // cols
         + (2 * cols - 2 - x) // cols
@@ -238,41 +228,28 @@
                     semaphore, inc=1, device_id=device, device_id_type=MESH
                 )
 
-    def ring(distance):
-        for dz in range(-distance, distance + 1):
-            for dx in sorted({abs(dz) - distance, distance - abs(dz)}):
-                if abs(dx) < cols and abs(dz) < owners:
-                    there_x, there_u = x + dx, u + dz
-                    inside = (
-                        (there_x >= 0)
-                        & (there_x < cols)
-                        & (there_u >= 0)
-                        & (there_u < owners)
-                    )
-                    yield inside, there_x * owners + there_u, {
-                        "blk": there_x * CORES + parity,
-                        "ulysses": there_u,
-                    }
-
-    farthest = cols + owners - 2
+    def hops(to_b, to_u):
+        return (
+            jnp.abs(to_b // CORES - x) + jnp.abs(to_b % CORES - parity) + jnp.abs(to_u - u)
+        )
+
+    reach = max(max(high - 1, owners - 1 - low) + cols, owners - 1)
     barrier = pltpu.get_barrier_semaphore()
     tell(barrier)
-    pl.semaphore_signal(barrier, inc=1, device_id=partner, device_id_type=MESH)
-    pl.semaphore_wait(barrier, near + 1)
-    if farthest > 1:
-        tell(level_sem.at[2])
+    pl.semaphore_wait(barrier, near)
+    tell(level_sem.at[2])
 
     for first, gain, part in ((query_in, query_gain, 0), (key_in, key_gain, 1)):
         loads[2 * part].wait()
         loads[2 * part + 1].wait()
         values = first[...].astype(jnp.float32)
         normed = (values * row_scale(values) * gain[...]).astype(jnp.bfloat16)
-        for h in range(chips):
+        for h in range(heads):
             stage[h, part * rows : (part + 1) * rows] = normed[
                 :, h * HEAD_DIM : (h + 1) * HEAD_DIM
             ]
     loads[4].wait()
-    for h in range(chips):
+    for h in range(heads):
         stage[h, 2 * rows :] = value_in[:, h * HEAD_DIM : (h + 1) * HEAD_DIM]
 
     started = []
@@ -298,28 +275,26 @@
             dst_ref=target,
             send_sem=sem_out,
             recv_sem=sem_in,
-            device_id=partner,
+            device_id={"blk": x * CORES + (1 - parity)},
             device_id_type=MESH,
         ).wait_recv()
 
-    send(
-        stage.at[me, pl.ds(rows, 2 * rows)],
-        passed.at[me],
-        pass_send.at[me],
-        pass_recv.at[me],
-        partner,
-    )
-    for distance in range(1, farthest + 1):
+    hosts = [(h, h // wide, low + h % wide) for h in range(heads)]
+    for distance in range(1, reach + 1):
         if distance > 1:
             pl.semaphore_wait(level_sem.at[distance], near)
-            if distance < farthest:
+            if distance < reach:
                 tell(level_sem.at[distance + 1])
-        for inside, there, device in ring(distance):
-
-            @pl.when(inside)
+        for h, to_b, to_u in hosts:
+
+            @pl.when(hops(to_b, to_u) == distance)
             def _():
                 remote(
-                    stage.at[there], landed.at[me], send_sem.at[there], recv_sem.at[me], device
+                    stage.at[h],
+                    landed.at[me],
+                    send_sem.at[h],
+                    recv_sem.at[me],
+                    {"blk": to_b, "ulysses": to_u},
                 ).start()
 
     loads[5].wait()
@@ -342,79 +317,63 @@
             slab_recv.at[u],
             {"ulysses": there},
         )
-    landed[me] = stage[me]
     slabs_in[u] = slabs_out[u]
 
-    for distance in range(1, farthest + 1):
-        for inside, there, _ in ring(distance):
-
-            @pl.when(inside)
+    order = [
+        (to_b, to_u)
+        for to_u in sorted(range(owners), key=lambda at: (low <= at < high, at))
+        for to_b in range(blks)
+    ]
+    factor = HEAD_DIM ** (-0.5) * math.log2(math.e)
+
+    @pl.when(hosting)
+    def _():
+        landed[me] = stage[own]
+        for to_b, to_u in order:
+            there = to_b * owners + to_u
+
+            @pl.when(there != me)
             def _():
-                arrive(landed.at[there], pass_send.at[0], recv_sem.at[there])
-                remote(
-                    landed.at[there, pl.ds(rows, 2 * rows)],
-                    passed.at[there],
-                    pass_send.at[there],
-                    pass_recv.at[there],
-                    partner,
-                ).start()
-
-    for there in [me] + [t for t, _ in reversed(others)]:
-        arrive(passed.at[there], pass_send.at[0], pass_recv.at[there])
-
-    count = chips * rows
-    keys = jnp.concatenate(
-        [
-            landed[:, rows : 2 * rows].reshape(count, HEAD_DIM),
-            passed[:, :rows].reshape(count, HEAD_DIM),
-        ],
-        axis=0,
-    )
-    mix = jnp.concatenate(
-        [
-            landed[:, 2 * rows :].reshape(count, HEAD_DIM),
-            passed[:, rows:].reshape(count, HEAD_DIM),
-        ],
-        axis=0,
-    )
-    factor = HEAD_DIM ** (-0.5) * math.log2(math.e)
-    targets = others + [(me, None)]
-    group = max(1, chips // GROUPS)
-    waiting = []
-
-    def flush():
-        for there, device, at in waiting:
-            send(
-                mixed_out.at[there],
-                attended.at[me],
-                back_send.at[at],
-                back_recv.at[me],
-                device,
+                arrive(landed.at[there], back_send.at[0], recv_sem.at[there])
+
+        count = devices * rows
+        keys = landed[:, rows : 2 * rows].reshape(count, HEAD_DIM)
+        mix = landed[:, 2 * rows :].reshape(count, HEAD_DIM)
+        group = devices // GROUPS
+
+        def flush(base):
+            for to_b, to_u in order[base : base + group]:
+                there = to_b * owners + to_u
+
+                @pl.when(there != me)
+                def _():
+                    remote(
+                        mixed_out.at[there],
+                        attended.at[own],
+                        back_send.at[there],
+                        back_recv.at[own],
+                        {"blk": to_b, "ulysses": to_u},
+                    ).start()
+
+        for base in range(0, devices, group):
+            part = [to_b * owners + to_u for to_b, to_u in order[base : base + group]]
+            queries = jnp.concatenate([landed[there, :rows] for there in part], axis=0)
+            scores = lax.dot_general(
+                queries, keys, (((1,), (1,)), ((), ())), preferred_element_type=jnp.float32
             )
-        waiting.clear()
-
-    for base in range(0, chips, group):
-        part = targets[base : base + group]
-        queries = jnp.concatenate([landed[there, :rows] for there, _ in part], axis=0)
-        scores = lax.dot_general(
-            queries, keys, (((1,), (1,)), ((), ())), preferred_element_type=jnp.float32
-        )
-        peak = jnp.max(scores, axis=-1, keepdims=True)
-        expo = jnp.exp2((scores - peak) * factor)
-        totals = jnp.sum(expo, axis=-1, keepdims=True)
-        output = jnp.dot(
-            expo.astype(jnp.bfloat16), mix, preferred_element_type=jnp.float32
-        )
-        output = (output * (1.0 / totals)).astype(jnp.bfloat16)
-        flush()
-        for at, (there, device) in enumerate(part):
-            piece = output[at * rows : (at + 1) * rows]
-            if device is None:
-                attended[there] = piece
-            else:
-                mixed_out[there] = piece
-                waiting.append((there, device, base + at))
-    flush()
+            peak = jnp.max(scores, axis=-1, keepdims=True)
+            expo = jnp.exp2((scores - peak) * factor)
+            totals = jnp.sum(expo, axis=-1, keepdims=True)
+            output = jnp.dot(
+                expo.astype(jnp.bfloat16), mix, preferred_element_type=jnp.float32
+            )
+            output = (output * (1.0 / totals)).astype(jnp.bfloat16)
+            if base:
+                flush(base - group)
+            for at, there in enumerate(part):
+                mixed_out[there] = output[at * rows : (at + 1) * rows]
+        flush(devices - group)
+        attended[own] = mixed_out[me]
 
     loads[6].wait()
     loads[7].wait()
@@ -427,44 +386,61 @@
     ).astype(jnp.bfloat16)
     hint[...] = placed.astype(jnp.float32) * gains[pl.ds(layer_smem[0], 1), :]
 
-    for there, _ in reversed(others):
-        arrive(attended.at[there], back_send.at[0], back_recv.at[there])
-    for h in range(chips):
+    for h, to_b, to_u in hosts:
+
+        @pl.when(hops(to_b, to_u) > 0)
+        def _():
+            arrive(attended.at[h], back_send.at[0], back_recv.at[h])
+            remote(
+                stage.at[h], landed.at[me], send_sem.at[h], recv_sem.at[me], around[0][1]
+            ).wait_send()
+
+    for h in range(heads):
         columns = slice(h * HEAD_DIM, (h + 1) * HEAD_DIM)
         out_ref[:, columns] = (attended[h].astype(jnp.float32) + hint[:, columns]).astype(
             jnp.bfloat16
         )
-    for there, device in others:
-        started.append(
-            remote(stage.at[there], landed.at[me], send_sem.at[there], recv_sem.at[me], device)
-        )
-        started.append(
-            remote(
-                landed.at[there, pl.ds(rows, 2 * rows)],
-                passed.at[there],
-                pass_send.at[there],
-                pass_recv.at[there],
-                partner,
-            )
-        )
     for copy in started:
         copy.wait_send()
 
-
-GROUPS = 2
+    @pl.when(hosting)
+    def _():
+        for there in range(devices):
+
+            @pl.when(there != me)
+            def _():
+                remote(
+                    mixed_out.at[there],
+                    attended.at[own],
+                    back_send.at[there],
+                    back_recv.at[own],
+                    around[0][1],
+                ).wait_send()
+
+
+GROUPS = 4
+
+
+def host_range(owners):
+    low = owners // 4
+    return (low, owners - low)
 
 
 def run(blks, owners, *arrays):
     query_proj, control, hint_weight, hint_gain = arrays[0], arrays[5], arrays[6], arrays[7]
     rows, feats = query_proj.shape
-    chips = blks // CORES * owners
+    low, high = host_range(owners)
+    heads = blks * (high - low)
+    devices = blks * owners
     fits = (
         blks % CORES == 0
-        and chips * HEAD_DIM == feats
+        and owners > 1
+        and heads * HEAD_DIM == feats
+        and devices % GROUPS == 0
         and rows % 16 == 0
         and rows % owners == 0
         and (rows // owners) % 8 == 0
-        and rows * chips <= 1024
+        and rows * devices <= 1024
     )
     if not fits:
         return shards(*arrays)
@@ -493,24 +469,21 @@
             pltpu.VMEM(hint_weight.shape, half),
             pltpu.VMEM(hint_gain.shape, wide),
             pltpu.SMEM((1, owners), jnp.int32),
-            pltpu.VMEM((chips, 3 * rows, HEAD_DIM), half),
-            pltpu.VMEM((chips, 3 * rows, HEAD_DIM), half),
-            pltpu.VMEM((chips, 2 * rows, HEAD_DIM), half),
+            pltpu.VMEM((heads, 3 * rows, HEAD_DIM), half),
+            pltpu.VMEM((devices, 3 * rows, HEAD_DIM), half),
             pltpu.VMEM((owners, rows // owners, inner), half),
             pltpu.VMEM((owners, rows // owners, inner), half),
-            pltpu.VMEM((chips, rows, HEAD_DIM), half),
-            pltpu.VMEM((chips, rows, HEAD_DIM), half),
+            pltpu.VMEM((devices, rows, HEAD_DIM), half),
+            pltpu.VMEM((heads, rows, HEAD_DIM), half),
             pltpu.VMEM((rows, feats), wide),
             dma((len(operands),)),
-            dma((chips,)),
-            dma((chips,)),
-            dma((chips,)),
-            dma((chips,)),
+            dma((heads,)),
+            dma((devices,)),
             dma((owners,)),
             dma((owners,)),
-            dma((chips,)),
-            dma((chips,)),
-            pltpu.SemaphoreType.REGULAR((blks // CORES + owners,)),
+            dma((devices,)),
+            dma((heads,)),
+            pltpu.SemaphoreType.REGULAR((blks // CORES + owners + 1,)),
         ],
         compiler_params=pltpu.CompilerParams(
             collective_id=0, has_side_effects=True, vmem_limit_bytes=16 << 20

time: 18.8 us -> 17.7 us (0.941)
  Pallas kernels: 17.4 us -> 16.3 us
    pallas_call x1, Pallas kernels: 17.4 us -> 16.3 us  [run(): pl.pallas_call(functools.partial(kernel, blks, owners), out_shape=jax.Sha...]
where the time goes in v4:
time: 17.7 us; the launch traced here: 17.6 us
  Pallas kernels  16.3 us (92%)
  between operations  0.66 us (4%)
  local copies, waits for them, and re-layouts  0.63 us (4%)
    pallas_call x1, Pallas kernels, run(): pl.pallas_call(functools.partial(kernel, blks, owners), out_shape=jax.Sha...  16.3 us
    unnamed x1, local copies, waits for them, and re-layouts  0.63 us

profile of v4, /device:TPU:0, one launch (start us, length us, event | category | flops | bytes accessed | tf_op | source)
XLA Modules:
  0.0 17.6 jit_solution(4159481126746549707)
XLA Ops:
  0.7 16.3 %shard_map.100 = bf16[32,1024]{1,0:T(8,128)(2,1)S(1)} custom-call(bf16[32,1024]{1,0:T(8,128)(2,1)} %query_hbm.1, bf16[32,1024]{1,0:T(8,128)(2,1)} %key_hbm.1, bf16[32,1024]{1,0:T(8,128)(2,1)} %value_hbm.1, f32[1,1024]{1,0:T(1,128)} %bitcast.2, f32[1,1024]{1,0:T(1,128)} %bitcast.3, bf16[32,384]{1,0:T(8,128)(2,1)} %control_hbm.1, ...), custom_call_target="tpu_custom_call" | custom-call | tf_op jit(solution)/shard_map/pallas_call | solution.py:456
  17.0 0.6 %copy.13 = bf16[32,1024]{1,0:T(8,128)(2,1)} copy(bf16[32,1024]{1,0:T(8,128)(2,1)S(1)} %shard_map.100) | data formatting | bytes 131072

commit v5 on v4

--- a/solution.py
+++ b/solution.py
@@ -182,7 +182,7 @@
     parity = lax.rem(b, CORES)
     x = b // CORES
     me = b * owners + u
-    own = b * wide + u - low
+    own = b * wide + lax.rem(u - low + wide * owners, wide)
     hosting = (u >= low) & (u < high)
 
     loads = [
@@ -230,7 +230,7 @@
 
     def hops(to_b, to_u):
         return (
-            jnp.abs(to_b // CORES - x) + jnp.abs(to_b % CORES - parity) + jnp.abs(to_u - u)
+            jnp.abs(to_b // CORES - x) + jnp.abs(lax.rem(jnp.int32(to_b), CORES) - parity) + jnp.abs(to_u - u)
         )
 
     reach = max(max(high - 1, owners - 1 - low) + cols, owners - 1)
@@ -285,7 +285,9 @@
             pl.semaphore_wait(level_sem.at[distance], near)
             if distance < reach:
                 tell(level_sem.at[distance + 1])
-        for h, to_b, to_u in hosts:
+        for _, base_b, to_u in hosts:
+            to_b = lax.rem(b + base_b, blks)
+            h = to_b * wide + to_u - low
 
             @pl.when(hops(to_b, to_u) == distance)
             def _():
@@ -418,7 +420,7 @@
                 ).wait_send()
 
 
-GROUPS = 4
+GROUPS = 8
 
 
 def host_range(owners):

time: 17.7 us -> 17.8 us (level)
  no operation moved by 1% of the time
where the time goes in v5:
time: 17.8 us; the launch traced here: 17.6 us
  Pallas kernels  16.3 us (92%)
  between operations  0.66 us (4%)
  local copies, waits for them, and re-layouts  0.63 us (4%)
    pallas_call x1, Pallas kernels, run(): pl.pallas_call(functools.partial(kernel, blks, owners), out_shape=jax.Sha...  16.3 us
    unnamed x1, local copies, waits for them, and re-layouts  0.63 us

profile of v5, /device:TPU:0, one launch (start us, length us, event | category | flops | bytes accessed | tf_op | source)
XLA Modules:
  0.0 17.6 jit_solution(7255882987744691145)
XLA Ops:
  0.7 16.3 %shard_map.100 = bf16[32,1024]{1,0:T(8,128)(2,1)S(1)} custom-call(bf16[32,1024]{1,0:T(8,128)(2,1)} %query_hbm.1, bf16[32,1024]{1,0:T(8,128)(2,1)} %key_hbm.1, bf16[32,1024]{1,0:T(8,128)(2,1)} %value_hbm.1, f32[1,1024]{1,0:T(1,128)} %bitcast.2, f32[1,1024]{1,0:T(1,128)} %bitcast.3, bf16[32,384]{1,0:T(8,128)(2,1)} %control_hbm.1, ...), custom_call_target="tpu_custom_call" | custom-call | tf_op jit(solution)/shard_map/pallas_call | solution.py:458
  17.0 0.6 %copy.13 = bf16[32,1024]{1,0:T(8,128)(2,1)} copy(bf16[32,1024]{1,0:T(8,128)(2,1)S(1)} %shard_map.100) | data formatting | bytes 131072
